TPU v7x, 32 devices: a whole 2x2x4 slice. The times are simulated.
32 devices in a mesh: parts: 2 (over y), row: 4 (over z), frame: 4 (over x, core).
Axes of the slice: x: 2, y: 2, z: 4, core: 2. Of those that a mesh axis runs over, the one named last changes fastest.
Arguments:
- latent: bfloat16 [8, 8, 16, 512], P(('parts', 'frame'), 'row'), parts along dimension 0, may hold values from -15 to 15
- qkv_weight: bfloat16 [3, 512, 512], P(None, 'frame'), may hold values from -0.125 to 0.125
- out_weight: bfloat16 [512, 512], P('frame'), may hold values from -0.25 to 0.25
- attn_gain: float32 [512], replicated, may hold values from 0.1 to 1.9
- in_weight: bfloat16 [512, 2, 2048], P(None, None, 'frame'), may hold values from -0.25 to 0.25
- depth_weight: float32 [3, 3, 2, 2048], replicated, may hold values from -2 to 2
- down_weight: bfloat16 [2048, 512], P('frame'), may hold values from -0.125 to 0.125
- mlp_gain: float32 [512], replicated, may hold values from 0.1 to 1.9
- conv_first: bfloat16 [3, 3, 3, 512, 512], P(None, None, None, 'frame'), may hold values from -0.0546875 to 0.0546875
- conv_second: bfloat16 [3, 3, 3, 512, 512], P(None, None, None, 'frame'), may hold values from -0.0546875 to 0.0546875
Outputs:
- decoded: bfloat16 [8, 8, 16, 512], P('parts', 'row', 'frame'), parts along dimension 0
There are 2 independent parts, one for each index of `parts`. A program takes and returns all parts, laid end to end along the dimension named above; an argument that names none is the same for every part. Nothing has to cross between parts.
All inputs are finite; a program needn't handle non-finite values.
Results may differ from a plain program's by a relative error of at most 0.015.
Values may be sent and summed in bfloat16 or wider, within the bound.
A program may use at most 128 MiB of HBM per device.

v0:
```python
import jax
import jax.numpy as jnp
from jax import lax
from jax.sharding import PartitionSpec as P

HEAD = 32


def padded_2(cells, sides, width):
    for axis, dim in sides:
        count = lax.axis_size(axis)
        ends = count - 1
        head = lax.slice_in_dim(cells, 0, width, axis=dim)
        tail = lax.slice_in_dim(cells, cells.shape[dim] - width, cells.shape[dim], axis=dim)
        cells = jnp.concatenate(
            [
                lax.ppermute(tail, axis, [(i, (i + 1) % count) for i in range(ends)]),
                cells,
                lax.ppermute(head, axis, [((i + 1) % count, i) for i in range(ends)]),
            ],
            axis=dim,
        )
    return cells


def norm_rows(values, gain):
    return values * lax.rsqrt(jnp.mean(values * values, axis=-1, keepdims=True) + 1e-05) * gain


def attend(packed):
    frames, height, columns = (packed.shape[0], packed.shape[1], packed.shape[2])
    width = packed.shape[4]
    heads = width // HEAD
    flat = packed.reshape(frames, height * columns, 3, heads, HEAD)
    query = jnp.maximum(flat[:, :, 0], 0)
    keys = jnp.maximum(flat[:, :, 1], 0)
    values = flat[:, :, 2]
    state = jnp.einsum("fnhd,fnhe->fhde", keys, values, preferred_element_type=jnp.float32)
    key_total = jnp.sum(keys.astype(jnp.float32), axis=1)
    state, key_total = (
        lax.psum(state.astype(jnp.bfloat16), "row").astype(jnp.float32),
        lax.psum(key_total.astype(jnp.bfloat16), "row").astype(jnp.float32),
    )
    count = height * lax.axis_size("row") * columns
    state = state / count
    key_mean = key_total / count
    query_wide = query.astype(jnp.float32)
    numer = jnp.einsum("fnhd,fhde->fnhe", query_wide, state, precision=lax.Precision.HIGHEST)
    denom = jnp.maximum(
        jnp.einsum("fnhd,fhd->fnh", query_wide, key_mean, precision=lax.Precision.HIGHEST), 1.0
    )
    return (numer / denom[..., None]).astype(jnp.bfloat16).reshape(frames, height, columns, width)


def depth_mix(inner, depth_local):
    height, columns = (inner.shape[1], inner.shape[2])
    extended = padded_2(inner, (("row", 1),), 1)
    padded = jnp.pad(extended, ((0, 0), (0, 0), (1, 1), (0, 0), (0, 0)))
    spread = jnp.zeros(inner.shape, jnp.float32)
    for shift_row in range(3):
        for shift_col in range(3):
            spread = (
                spread
                + padded[:, shift_row : shift_row + height, shift_col : shift_col + columns].astype(
                    jnp.float32
                )
                * depth_local[shift_row, shift_col]
            )
    return (spread[..., 0, :] * jax.nn.silu(spread[..., 1, :])).astype(jnp.bfloat16)


def conv_tile(extended, kernel):
    frames, padded_rows, columns, width = extended.shape
    height = padded_rows - 2
    out_width = kernel.shape[3]
    padded = jnp.pad(extended, ((1, 1), (0, 0), (1, 1), (0, 0)))
    result = jnp.zeros((frames * height * columns, out_width), jnp.float32)
    for shift_time in range(3):
        for shift_row in range(3):
            slab = padded[shift_time : shift_time + frames, shift_row : shift_row + height]
            stacked = jnp.stack(
                [slab[:, :, shift_col : shift_col + columns] for shift_col in range(3)], axis=3
            )
            result = result + jnp.einsum(
                "nci,coi->no",
                stacked.reshape(-1, 3, width),
                kernel[shift_time, shift_row],
                preferred_element_type=jnp.float32,
            )
    return result.reshape(frames, height, columns, out_width)


def local(
    latent,
    qkv_weight,
    out_weight,
    attn_gain,
    in_weight,
    depth_weight,
    down_weight,
    mlp_gain,
    conv_first,
    conv_second,
):
    frames, height, columns, width = latent.shape
    place = lax.axis_index("frame")
    packed = jnp.einsum(
        "frwc,kjc->frwkj",
        latent,
        lax.all_gather(qkv_weight, "frame", axis=1, tiled=True),
        preferred_element_type=jnp.float32,
    ).astype(jnp.bfloat16)
    mixed = attend(packed)
    section = mixed
    attn_out = jnp.einsum(
        "frwj,jc->frwc",
        section,
        lax.all_gather(out_weight, "frame", axis=0, tiled=True),
        preferred_element_type=jnp.float32,
    )
    first = (latent.astype(jnp.float32) + norm_rows(attn_out, attn_gain)).astype(jnp.bfloat16)
    inner = jax.nn.silu(
        jnp.einsum(
            "frwc,ckj->frwkj",
            first,
            lax.all_gather(in_weight, "frame", axis=2, tiled=True),
            preferred_element_type=jnp.float32,
        )
    ).astype(jnp.bfloat16)
    gated = depth_mix(inner, depth_weight)
    section = gated
    mlp_out = jnp.einsum(
        "frwj,jc->frwc",
        section,
        lax.all_gather(down_weight, "frame", axis=0, tiled=True),
        preferred_element_type=jnp.float32,
    )
    second = (first.astype(jnp.float32) + norm_rows(mlp_out, mlp_gain)).astype(jnp.bfloat16)
    gathered = lax.all_gather(second, "frame", axis=0, tiled=True)
    out_share = conv_first.shape[3]
    extended = padded_2(gathered, (("row", 1),), 2)
    activated = jax.nn.silu(conv_tile(extended, conv_first))
    global_row = lax.axis_index("row") * height - 1 + lax.iota(jnp.int32, height + 2)
    inside = ((global_row >= 0) & (global_row < height * lax.axis_size("row"))).astype(jnp.float32)
    hidden_conv = (activated * inside[None, :, None, None]).astype(jnp.bfloat16)
    joined = lax.all_gather(hidden_conv, "frame", axis=3, tiled=True)
    result = conv_tile(joined, conv_second)
    own_part = lax.dynamic_slice_in_dim(gathered, place * out_share, out_share, 3)
    final = (own_part.astype(jnp.float32) + result).astype(jnp.bfloat16)
    return lax.all_to_all(final, "frame", split_axis=2, concat_axis=3, tiled=True)


def solution(mesh):
    in_specs = (
        P(("parts", "frame"), "row", None, None),
        P(None, "frame", None),
        P("frame", None),
        P(),
        P(None, None, "frame"),
        P(),
        P("frame", None),
        P(),
        P(None, None, None, "frame", None),
        P(None, None, None, "frame", None),
    )
    out_specs = P("parts", "row", "frame", None)
    return jax.shard_map(local, mesh=mesh, in_specs=in_specs, out_specs=out_specs, check_vma=False)
```

profile of v0, /device:TPU:0, one launch (start us, length us, event | category | flops | bytes accessed | tf_op | source)
XLA Modules:
  0.0 137.9 jit_solution(649510478248561732)
XLA Ops:
  6.5 0.7 all-gather.4.cloned.1.call-update
  7.3 0.0 all-gather.6.cloned.1.call-start
  7.3 2.4 %copy.34 = bf16[512,2,512]{2,0,1:T(8,128)(2,1)} copy(bf16[512,2,512]{2,1,0:T(2,128)(2,1)} %param.14) | data formatting | bytes 2097152 | tf_op args[4]
  9.7 0.0 all-gather.6.cloned.1.call-update
  9.7 0.0 all-gather.8.cloned.1.call-start
  9.8 0.7 all-gather.8.cloned.1.call-update
  10.5 8.6 %all_gather.19 = bf16[512,512]{1,0:T(8,128)(2,1)S(1)} all-gather(bf16[128,512]{1,0:T(8,128)(2,1)S(1)} %copy-done.1), channel_id=1, replica_groups=mesh['parts'=2,'row'=4,'frame'=4] {'frame'}, dimensions={0}, use_global_device_ids=true | all-gather | bytes 655360 | tf_op jit(solution)/shard_map/all_gather | solution.py:118
  19.1 12.1 %all-gather.4.cloned.1.call-done = bf16[3,512,512]{2,1,0:T(8,128)(2,1)} async-done(((bf16[3,128,512]{2,1,0:T(8,128)(2,1)}), bf16[3,512,512]{2,1,0:T(8,128)(2,1)}) %all-gather.4.cloned.1.call-update) | async-done | bytes 1572880 | tf_op jit(solution)/shard_map/all_gather | solution.py:110
  31.3 2.0 %fusion.7 = bf16[2,16,3,512]{3,1,2,0:T(8,128)(2,1)S(1)} fusion(bf16[3,512,512]{2,1,0:T(8,128)(2,1)} %all-gather.4.cloned.1.call-done, bf16[1,2,16,512]{3,2,1,0:T(8,128)(2,1)S(1)} %copy-done.2), kind=kOutput, calls=%fused_computation.59 | convolution fusion | flops 50380800 | bytes 1703936 | tf_op jit(solution)/shard_map/frwc,kjc->frwkj/dot_general | solution.py:107
  33.3 0.2 reshape.298
  33.5 0.2 copy.44
  33.7 0.1 maximum_reduce_fusion
  33.8 0.2 fusion.10
  34.0 21.4 %all-reduce.3 = (bf16[1,16,32,32]{3,2,1,0:T(8,128)(2,1)S(1)}, bf16[1,16,32]{2,1,0:T(8,128)(2,1)S(1)}) all-reduce(bf16[1,16,32,32]{3,2,1,0:T(8,128)(2,1)S(1)} %fusion.10, bf16[1,16,32]{2,1,0:T(8,128)(2,1)S(1)} %bitcast.373), channel_id=1, replica_groups=mesh['parts'=2,'row'=4,'frame'=4] {'row'}, use_global_device_ids=true, to_apply=%region_0.0 | all-reduce | flops 16896 | bytes 67584 | tf_op jit(solution)/shard_map/psum | solution.py:41
  55.4 0.2 copy.46
  55.6 0.2 fusion.174
  55.8 0.4 fusion.28
  56.2 0.2 copy.33
  56.4 0.2 reshape.302
  56.6 0.3 multiply_reduce_fusion.1
  56.9 0.1 fusion.184
  57.0 10.4 %all-gather.6.cloned.1.call-done = bf16[512,2,2048]{2,0,1:T(8,128)(2,1)} async-done(((bf16[512,2,512]{2,0,1:T(8,128)(2,1)}), bf16[512,2,2048]{2,0,1:T(8,128)(2,1)}) %all-gather.6.cloned.1.call-update) | async-done | bytes 4194320 | tf_op jit(solution)/shard_map/all_gather | solution.py:126
  67.3 3.0 %multiply_convert_fusion = bf16[2,16,2,2048]{3,1,2,0:T(8,128)(2,1)S(1)} fusion(bf16[512,2,2048]{2,0,1:T(8,128)(2,1)} %all-gather.6.cloned.1.call-done, bf16[1,2,16,512]{3,2,1,0:T(8,128)(2,1)S(1)} %fusion.184), kind=kOutput, calls=%fused_computation.154 | convolution fusion | flops 134873088 | bytes 4489216 | tf_op jit(solution)/shard_map/frwc,ckj->frwkj/dot_general | solution.py:123
  70.4 3.4 %collective-permute-start = (bf16[1,1,16,2,2048]{4,2,3,1,0:T(8,128)(2,1)S(1)}, bf16[1,1,16,2,2048]{4,2,3,1,0:T(8,128)(2,1)S(1)}, u32[]{:S(2)}, u32[]{:S(2)}) collective-permute-start(bf16[1,1,16,2,2048]{4,2,3,1,0:T(8,128)(2,1)S(1)} %get-tuple-element.62), channel_id=1, source_target_pairs={{0,4},{4,8},{8,12},{1,5},{5,9},{9,13},{2,6},{6,10},{10,14},{3,7},{... | collective-permute-start | bytes 393224 | tf_op jit(solution)/shard_map/ppermute | solution.py:17
  73.8 1.3 collective-permute-start.1
  75.1 1.8 %collective-permute-done = bf16[1,1,16,2,2048]{4,2,3,1,0:T(8,128)(2,1)S(1)} collective-permute-done((bf16[1,1,16,2,2048]{4,2,3,1,0:T(8,128)(2,1)S(1)}, bf16[1,1,16,2,2048]{4,2,3,1,0:T(8,128)(2,1)S(1)}, u32[]{:S(2)}, u32[]{:S(2)}) %collective-permute-start) | collective-permute-done | bytes 131104 | tf_op jit(solution)/shard_map/ppermute | solution.py:17
  76.9 4.1 %collective-permute-done.1 = bf16[1,1,16,2,2048]{4,2,3,1,0:T(8,128)(2,1)S(1)} collective-permute-done((bf16[1,1,16,2,2048]{4,2,3,1,0:T(8,128)(2,1)S(1)}, bf16[1,1,16,2,2048]{4,2,3,1,0:T(8,128)(2,1)S(1)}, u32[]{:S(2)}, u32[]{:S(2)}) %collective-permute-start.1) | collective-permute-done | bytes 131104 | tf_op jit(solution)/shard_map/ppermute | solution.py:19
  81.1 0.3 fusion.33
  81.3 0.5 fusion.82
  81.8 9.7 %all-gather.8.cloned.1.call-done = bf16[2048,512]{1,0:T(8,128)(2,1)} async-done(((bf16[512,512]{1,0:T(8,128)(2,1)}), bf16[2048,512]{1,0:T(8,128)(2,1)}) %all-gather.8.cloned.1.call-update) | async-done | bytes 2097168 | tf_op jit(solution)/shard_map/all_gather | solution.py:135
  91.5 2.1 %multiply_reduce_fusion = (f32[2,16]{1,0:T(2,128)S(1)}, f32[2,16,512]{2,1,0:T(8,128)S(1)}) fusion(bf16[2048,512]{1,0:T(8,128)(2,1)} %all-gather.8.cloned.1.call-done, f32[1,2,16,2,2048]{4,2,3,1,0:T(8,128)S(1)} %fusion.82), kind=kOutput, calls=%fused_computation.264 | convolution fusion | flops 67534816 | bytes 2687104 | tf_op jit(solution)/shard_map/frwj,jc->frwc/dot_general | solution.py:132
  93.6 0.1 fusion.183
  93.7 5.4 %all_gather.22 = bf16[4,2,16,512]{3,2,1,0:T(8,128)(2,1)S(1)} all-gather(bf16[1,2,16,512]{3,2,1,0:T(8,128)(2,1)S(1)} %fusion.183), channel_id=1, replica_groups=mesh['parts'=2,'row'=4,'frame'=4] {'frame'}, dimensions={0}, use_global_device_ids=true | all-gather | bytes 163840 | tf_op jit(solution)/shard_map/all_gather | solution.py:139
  99.1 3.4 %collective-permute-start.2 = (bf16[4,2,16,512]{3,2,1,0:T(8,128)(2,1)S(1)}, bf16[4,2,16,512]{3,2,1,0:T(8,128)(2,1)S(1)}, u32[]{:S(2)}, u32[]{:S(2)}) collective-permute-start(bf16[4,2,16,512]{3,2,1,0:T(8,128)(2,1)S(1)} %all_gather.22), channel_id=1, source_target_pairs={{0,4},{4,8},{8,12},{1,5},{5,9},{9,13},{2,6},{6,10},{10,14},{3,7},{... | collective-permute-start | bytes 393224 | tf_op jit(solution)/shard_map/ppermute | solution.py:17
  102.5 1.3 collective-permute-start.3
  103.8 1.9 %collective-permute-done.2 = bf16[4,2,16,512]{3,2,1,0:T(8,128)(2,1)S(1)} collective-permute-done((bf16[4,2,16,512]{3,2,1,0:T(8,128)(2,1)S(1)}, bf16[4,2,16,512]{3,2,1,0:T(8,128)(2,1)S(1)}, u32[]{:S(2)}, u32[]{:S(2)}) %collective-permute-start.2) | collective-permute-done | bytes 131104 | tf_op jit(solution)/shard_map/ppermute | solution.py:17
  105.8 4.1 %collective-permute-done.3 = bf16[4,2,16,512]{3,2,1,0:T(8,128)(2,1)S(1)} collective-permute-done((bf16[4,2,16,512]{3,2,1,0:T(8,128)(2,1)S(1)}, bf16[4,2,16,512]{3,2,1,0:T(8,128)(2,1)S(1)}, u32[]{:S(2)}, u32[]{:S(2)}) %collective-permute-start.3) | collective-permute-done | bytes 131104 | tf_op jit(solution)/shard_map/ppermute | solution.py:19
  109.9 0.8 pad_slice_fusion.23
  110.7 0.2 fusion.213
  110.9 1.0 copy-done.5
  111.9 0.4 convolution_bitcast_fusion.8
  112.3 0.4 convolution_bitcast_fusion.7
  112.7 0.4 convolution_bitcast_fusion.6
  113.1 0.4 convolution_bitcast_fusion.5
  113.4 0.4 convolution_bitcast_fusion.4
  113.8 0.4 convolution_bitcast_fusion.3
  114.2 0.4 convolution_bitcast_fusion.2
  114.5 0.4 convolution_bitcast_fusion.1
  114.9 0.4 fusion.18
  115.3 0.1 multiply_convert_fusion.1
  115.4 5.9 %all_gather.23 = bf16[4,4,16,512]{3,2,1,0:T(8,128)(2,1)S(1)} all-gather(bf16[4,4,16,128]{3,2,1,0:T(8,128)(2,1)S(1)} %multiply_convert_fusion.1), channel_id=1, replica_groups=mesh['parts'=2,'row'=4,'frame'=4] {'frame'}, dimensions={3}, use_global_device_ids=true | all-gather | bytes 327680 | tf_op jit(solution)/shard_map/all_gather | solution.py:146
  121.3 0.3 pad_slice_fusion.47
  121.7 0.1 fusion.215
  121.8 0.3 convolution_bitcast_fusion.17
  122.1 0.3 convolution_bitcast_fusion.16
  122.4 0.3 convolution_bitcast_fusion.15
  122.6 0.3 convolution_bitcast_fusion.14
  122.9 0.3 convolution_bitcast_fusion.13
  123.2 0.3 convolution_bitcast_fusion.12
  123.5 0.3 convolution_bitcast_fusion.11
  123.7 0.3 convolution_bitcast_fusion.10
  124.0 0.3 fusion.26
  124.4 6.3 %all_to_all.18 = bf16[4,2,16,128]{3,1,0,2:T(2,128)(2,1)S(1)} all-to-all(bf16[4,2,16,128]{3,1,0,2:T(2,128)(2,1)S(1)} %copy.36), channel_id=1, replica_groups=mesh['parts'=2,'row'=4,'frame'=4] {'frame'}, dimensions={2} | all-to-all | bytes 65536 | tf_op jit(solution)/shard_map/all_to_all | solution.py:150
  130.7 0.6 all_to_all.16
  (30 shorter events, 0.3 us)
Async XLA Ops:
  6.5 4.0 %copy-start.1 = (bf16[128,512]{1,0:T(8,128)(2,1)S(1)}, bf16[128,512]{1,0:T(8,128)(2,1)}, u32[]{:S(2)}) copy-start(bf16[128,512]{1,0:T(8,128)(2,1)} %param.12) | copy-start | bytes 393220
  6.5 24.7 %copy-start.2 = (bf16[1,2,16,512]{3,2,1,0:T(8,128)(2,1)S(1)}, bf16[1,2,16,512]{3,2,1,0:T(8,128)(2,1)}, u32[]{:S(2)}) copy-start(bf16[1,2,16,512]{3,2,1,0:T(8,128)(2,1)} %param.10) | copy-start | bytes 98308
  6.5 24.7 %all-gather.4.cloned.1.call-start = ((), (), s32[]{:S(2)}) async-start(), calls=%async_computation.1 | async-start | bytes 1966080 | tf_op jit(solution)/shard_map/all_gather | solution.py:110
  7.3 60.1 %all-gather.6.cloned.1.call-start = ((), (), s32[]{:S(2)}) async-start(), calls=%async_computation.2 | async-start | bytes 5242880 | tf_op jit(solution)/shard_map/all_gather | solution.py:126
  9.7 81.7 %all-gather.8.cloned.1.call-start = ((), (), s32[]{:S(2)}) async-start(), calls=%async_computation.3 | async-start | bytes 2621440 | tf_op jit(solution)/shard_map/all_gather | solution.py:135
  19.1 37.7 %copy-start.3 = (f32[512]{0:T(512)S(1)}, f32[512]{0:T(512)}, u32[]{:S(2)}) copy-start(f32[512]{0:T(512)} %param.13) | copy-start | bytes 6148
  56.9 18.2 %copy-start = (f32[3,3,2,2048]{3,2,1,0:T(2,128)S(1)}, f32[3,3,2,2048]{3,2,1,0:T(2,128)}, u32[]{:S(2)}) copy-start(f32[3,3,2,2048]{3,2,1,0:T(2,128)} %param.15) | copy-start | bytes 442372
  70.4 6.5 %collective-permute-start = (bf16[1,1,16,2,2048]{4,2,3,1,0:T(8,128)(2,1)S(1)}, bf16[1,1,16,2,2048]{4,2,3,1,0:T(8,128)(2,1)S(1)}, u32[]{:S(2)}, u32[]{:S(2)}) collective-permute-start(bf16[1,1,16,2,2048]{4,2,3,1,0:T(8,128)(2,1)S(1)} %get-tuple-element.62), channel_id=1, source_target_pairs={{0,4},{4,8},{8,12},{1,5},{5,9},{9,13},{2,6},{6,10},{10,14},{3,7},{... | collective-permute-start | bytes 393224 | tf_op jit(solution)/shard_map/ppermute | solution.py:17
  73.8 7.3 %collective-permute-start.1 = (bf16[1,1,16,2,2048]{4,2,3,1,0:T(8,128)(2,1)S(1)}, bf16[1,1,16,2,2048]{4,2,3,1,0:T(8,128)(2,1)S(1)}, u32[]{:S(2)}, u32[]{:S(2)}) collective-permute-start(bf16[1,1,16,2,2048]{4,2,3,1,0:T(8,128)(2,1)S(1)} %get-tuple-element.63), channel_id=1, source_target_pairs={{4,0},{8,4},{12,8},{5,1},{9,5},{13,9},{6,2},{10,6},{14,10},{7,3},{... | collective-permute-start | bytes 393224 | tf_op jit(solution)/shard_map/ppermute | solution.py:19
  75.1 18.4 %copy-start.4 = (f32[512]{0:T(512)S(1)}, f32[512]{0:T(512)}, u32[]{:S(2)}) copy-start(f32[512]{0:T(512)} %param.17) | copy-start | bytes 6148
  99.1 6.6 %collective-permute-start.2 = (bf16[4,2,16,512]{3,2,1,0:T(8,128)(2,1)S(1)}, bf16[4,2,16,512]{3,2,1,0:T(8,128)(2,1)S(1)}, u32[]{:S(2)}, u32[]{:S(2)}) collective-permute-start(bf16[4,2,16,512]{3,2,1,0:T(8,128)(2,1)S(1)} %all_gather.22), channel_id=1, source_target_pairs={{0,4},{4,8},{8,12},{1,5},{5,9},{9,13},{2,6},{6,10},{10,14},{3,7},{... | collective-permute-start | bytes 393224 | tf_op jit(solution)/shard_map/ppermute | solution.py:17
  102.5 7.4 %collective-permute-start.3 = (bf16[4,2,16,512]{3,2,1,0:T(8,128)(2,1)S(1)}, bf16[4,2,16,512]{3,2,1,0:T(8,128)(2,1)S(1)}, u32[]{:S(2)}, u32[]{:S(2)}) collective-permute-start(bf16[4,2,16,512]{3,2,1,0:T(8,128)(2,1)S(1)} %all_gather.22), channel_id=1, source_target_pairs={{4,0},{8,4},{12,8},{5,1},{9,5},{13,9},{6,2},{10,6},{14,10},{7,3},{... | collective-permute-start | bytes 393224 | tf_op jit(solution)/shard_map/ppermute | solution.py:19
  109.9 2.0 %copy-start.5 = (bf16[3,3,3,128,512]{4,3,2,1,0:T(8,128)(2,1)S(1)}, bf16[3,3,3,128,512]{4,3,2,1,0:T(8,128)(2,1)}, u32[]{:S(2)}) copy-start(bf16[3,3,3,128,512]{4,3,2,1,0:T(8,128)(2,1)} %param.18) | copy-start | bytes 10616836
  114.9 6.9 %copy-start.6 = (bf16[3,3,3,128,512]{4,3,2,1,0:T(8,128)(2,1)S(1)}, bf16[3,3,3,128,512]{4,3,2,1,0:T(8,128)(2,1)}, u32[]{:S(2)}) copy-start(bf16[3,3,3,128,512]{4,3,2,1,0:T(8,128)(2,1)} %param.19) | copy-start | bytes 10616836
Sparse Core Ops, SparseCore 0:
  8.9 22.3 all-gather.3
  32.8 34.4 all-gather.5
  68.9 22.5 all-gather.7
where the time goes:
time: 138 us
  blocking collectives  47.7 us (35%)
  waiting for transfers between devices  45.5 us (33%)
  matrix products  13.8 us (10%)
  between operations  13.6 us (10%)
  starting transfers between devices  9.45 us (7%)
  local copies, waits for them, and re-layouts  6.56 us (5%)
    psum x1, blocking collectives, attend(): lax.psum(state.astype(jnp.bfloat16), 'row').astype(jnp.float32)  21.4 us
    all_gather x1, waiting for transfers between devices, local(): lax.all_gather(qkv_weight, 'frame', axis=1, tiled=True)  12.1 us
    all_gather x1, waiting for transfers between devices, local(): lax.all_gather(in_weight, 'frame', axis=2, tiled=True)  10.4 us
    all_gather x1, waiting for transfers between devices, local(): lax.all_gather(down_weight, 'frame', axis=0, tiled=True)  9.69 us
    all_gather x1, blocking collectives, local(): lax.all_gather(out_weight, 'frame', axis=0, tiled=True)  8.65 us
    ppermute x2, waiting for transfers between devices, padded_2(): lax.ppermute(head, axis, [((i + 1) % count, i) for i in range(ends)])  8.23 us
    ppermute x2, starting transfers between devices, padded_2(): lax.ppermute(tail, axis, [(i, (i + 1) % count) for i in range(ends)])  6.78 us
    all_to_all x1, blocking collectives, local(): lax.all_to_all(final, 'frame', split_axis=2, concat_axis=3, tiled=True)  6.3 us
  transfers between devices with their start and end apart: 7, of which 7 were waited for; matrix products, arithmetic and copies ran while one was open for 8% of the time, Pallas kernels for 0%

commit v1 on v0

--- a/solution.py
+++ b/solution.py
@@ -4,6 +4,43 @@
 from jax.sharding import PartitionSpec as P
 
 HEAD = 32
+
+
+def edit_the_quarters(sample, pos_dim, array_in, k_dim):
+    block_out, response, outer = (
+        lax.axis_size("frame"),
+        lax.axis_index("frame"),
+        sample.shape[pos_dim],
+    )
+    buffers = [(h, (h + 1) % block_out) for h in range(block_out)]
+    inbox = [(ix, s) for s, ix in buffers]
+    o_now, built = (
+        lax.ppermute(sample, "frame", perm=buffers),
+        lax.ppermute(sample, "frame", inbox),
+    )
+    finding = array_in(sample, response * outer)
+    even = finding.shape[k_dim]
+    main = jnp.zeros(
+        (*finding.shape[:k_dim], block_out * even, *finding.shape[k_dim + 1 :]), finding.dtype
+    )
+
+    def _pack_area(main, finding, d_next):
+        passed = lax.dynamic_update_slice_in_dim(main, finding, d_next * even, axis=k_dim)
+        return passed
+
+    main = _pack_area(main, finding, response)
+    for m in range(1, block_out // 2 + 1):
+        y_new, current_arr = ((response - m) % block_out, (response + m) % block_out)
+        p_next = (o_now, built)
+        if m < block_out // 2:
+            o_now, built = (
+                lax.ppermute(o_now, "frame", perm=buffers),
+                lax.ppermute(built, "frame", perm=inbox),
+            )
+        main = _pack_area(main, array_in(p_next[0], y_new * outer), y_new)
+        if 2 * m < block_out:
+            main = _pack_area(main, array_in(p_next[1], current_arr * outer), current_arr)
+    return main
 
 
 def padded_2(cells, sides, width):
@@ -104,11 +141,13 @@
 ):
     frames, height, columns, width = latent.shape
     place = lax.axis_index("frame")
-    packed = jnp.einsum(
-        "frwc,kjc->frwkj",
-        latent,
-        lax.all_gather(qkv_weight, "frame", axis=1, tiled=True),
-        preferred_element_type=jnp.float32,
+    packed = edit_the_quarters(
+        qkv_weight,
+        1,
+        lambda part, at: jnp.einsum(
+            "frwc,kjc->frwkj", latent, part, preferred_element_type=jnp.float32
+        ),
+        4,
     ).astype(jnp.bfloat16)
     mixed = attend(packed)
     section = mixed

time: 138 us -> 130 us (0.942)
  waiting for transfers between devices: 45.5 us -> 27.2 us
  blocking collectives: 47.7 us -> 57.3 us
    ppermute x0 -> x3, waiting for transfers between devices: none -> 15.6 us  [the longest x1 15.5 us: edit_the_quarters(): lax.ppermute(o_now, 'frame', perm=buffers)]
    all_gather x1 -> x0, waiting for transfers between devices: 12.1 us -> none  [local(): lax.all_gather(qkv_weight, 'frame', axis=1, tiled=True)]
    all_gather x1, waiting for transfers between devices: 10.4 us -> 0.02 us  [local(): lax.all_gather(in_weight, 'frame', axis=2, tiled=True)]
    all_gather x1, waiting for transfers between devices: 9.69 us -> 0.02 us  [local(): lax.all_gather(down_weight, 'frame', axis=0, tiled=True)]
    all_gather x1, blocking collectives: 8.65 us -> 16.9 us  [local(): lax.all_gather(out_weight, 'frame', axis=0, tiled=True)]
    ppermute x0 -> x3, starting transfers between devices: none -> 2.87 us  [the longest x1 1.98 us: edit_the_quarters(): lax.ppermute(sample, 'frame', inbox)]
    ppermute x2, starting transfers between devices: 6.78 us -> 5.09 us  [padded_2(): lax.ppermute(tail, axis, [(i, (i + 1) % count) for i in range(ends)])]
    unnamed x19 -> x21, local copies, waits for them, and re-layouts: 3.87 us -> 3.89 us
  transfers between devices with their start and end apart: 7 -> 9, of which waited for: 7 -> 5; matrix products, arithmetic and copies ran while one was open for 8% -> 6% of each run, Pallas kernels for 0% -> 0%
where the time goes in v1:
time: 130 us
  blocking collectives  57.3 us (44%)
  waiting for transfers between devices  27.2 us (21%)
  between operations  13.9 us (11%)
  matrix products  12.9 us (10%)
  starting transfers between devices  10.6 us (8%)
  local copies, waits for them, and re-layouts  6.74 us (5%)
    psum x1, blocking collectives, attend(): lax.psum(state.astype(jnp.bfloat16), 'row').astype(jnp.float32)  22.4 us
    all_gather x1, blocking collectives, local(): lax.all_gather(out_weight, 'frame', axis=0, tiled=True)  16.9 us
    ppermute x1, waiting for transfers between devices, edit_the_quarters(): lax.ppermute(o_now, 'frame', perm=buffers)  15.5 us
    ppermute x2, waiting for transfers between devices, padded_2(): lax.ppermute(head, axis, [((i + 1) % count, i) for i in range(ends)])  8.47 us
    all_to_all x1, blocking collectives, local(): lax.all_to_all(final, 'frame', split_axis=2, concat_axis=3, tiled=True)  6.52 us
    all_gather x1, blocking collectives, local(): joined = lax.all_gather(hidden_conv, 'frame', axis=3, tiled=True)  6.06 us
    dot_general x18, matrix products, conv_tile(): jnp.einsum('nci,coi->no', stacked.reshape(-1, 3, width), kernel[shift_tim...  5.73 us
    all_gather x1, blocking collectives, local(): gathered = lax.all_gather(second, 'frame', axis=0, tiled=True)  5.42 us
  transfers between devices with their start and end apart: 9, of which 5 were waited for; matrix products, arithmetic and copies ran while one was open for 6% of the time, Pallas kernels for 0%

profile of v1, /device:TPU:0, one launch (start us, length us, event | category | flops | bytes accessed | tf_op | source)
XLA Modules:
  0.0 129.8 jit_solution(11087425191196350645)
XLA Ops:
  6.5 2.4 %copy.40 = bf16[512,2,512]{2,0,1:T(8,128)(2,1)} copy(bf16[512,2,512]{2,1,0:T(2,128)(2,1)} %param.14) | data formatting | bytes 2097152 | tf_op args[4]
  9.0 0.0 all-gather.5.cloned.1.call-start
  9.0 0.5 collective-permute-start
  9.6 2.0 %collective-permute-start.1 = (bf16[3,128,512]{2,1,0:T(8,128)(2,1)}, bf16[3,128,512]{2,1,0:T(8,128)(2,1)S(1)}, u32[]{:S(2)}, u32[]{:S(2)}) collective-permute-start(bf16[3,128,512]{2,1,0:T(8,128)(2,1)} %param.11), channel_id=1, source_target_pairs={{1,0},{2,1},{3,2},{0,3},{5,4},{6,5},{7,6},{4,7},{9,8},{10,9},{11,1... | collective-permute-start | bytes 1179656 | tf_op jit(solution)/shard_map/ppermute | solution.py:19
  11.6 0.2 convolution_bitcast_fusion.22
  11.9 16.9 %all_gather.15 = bf16[512,512]{1,0:T(8,128)(2,1)S(1)} all-gather(bf16[128,512]{1,0:T(8,128)(2,1)S(1)} %copy-done.3), channel_id=1, replica_groups=mesh['parts'=2,'row'=4,'frame'=4] {'frame'}, dimensions={0}, use_global_device_ids=true | all-gather | bytes 655360 | tf_op jit(solution)/shard_map/all_gather | solution.py:157
  28.8 0.3 collective-permute-start.2
  29.2 0.2 convolution_bitcast_fusion.21
  29.5 0.2 convolution_bitcast_fusion.20
  29.8 15.5 %collective-permute-done.2 = bf16[3,128,512]{2,1,0:T(8,128)(2,1)S(1)} collective-permute-done((bf16[3,128,512]{2,1,0:T(8,128)(2,1)S(1)}, bf16[3,128,512]{2,1,0:T(8,128)(2,1)S(1)}, u32[]{:S(2)}, u32[]{:S(2)}) %collective-permute-start.2) | collective-permute-done | bytes 393248 | tf_op jit(solution)/shard_map/ppermute | solution.py:37
  45.3 0.2 convolution_bitcast_fusion.19
  45.6 0.2 reshape.302
  45.8 0.2 copy.50
  46.0 0.1 maximum_reduce_fusion
  46.2 0.2 fusion.5
  46.3 22.4 %all-reduce.3 = (bf16[1,16,32,32]{3,2,1,0:T(8,128)(2,1)S(1)}, bf16[1,16,32]{2,1,0:T(8,128)(2,1)S(1)}) all-reduce(bf16[1,16,32,32]{3,2,1,0:T(8,128)(2,1)S(1)} %fusion.5, bf16[1,16,32]{2,1,0:T(8,128)(2,1)S(1)} %bitcast.394), channel_id=1, replica_groups=mesh['parts'=2,'row'=4,'frame'=4] {'row'}, use_global_device_ids=true, to_apply=%region_0.1 | all-reduce | flops 16896 | bytes 67584 | tf_op jit(solution)/shard_map/psum | solution.py:78
  68.7 0.2 copy.52
  68.9 0.2 fusion.173
  69.2 0.4 fusion.23
  69.6 0.2 copy.39
  69.7 0.2 reshape.306
  69.9 0.3 multiply_reduce_fusion.1
  70.2 0.1 fusion.183
  70.3 3.1 %multiply_convert_fusion = bf16[2,16,2,2048]{3,1,2,0:T(8,128)(2,1)S(1)} fusion(bf16[512,2,2048]{2,0,1:T(8,128)(2,1)} %all-gather.3.cloned.1.call-done, bf16[1,2,16,512]{3,2,1,0:T(8,128)(2,1)S(1)} %fusion.183), kind=kOutput, calls=%fused_computation.155 | convolution fusion | flops 134873088 | bytes 4489216 | tf_op jit(solution)/shard_map/frwc,ckj->frwkj/dot_general | solution.py:162
  73.5 1.3 collective-permute-start.3
  74.8 1.3 collective-permute-start.4
  76.1 1.2 collective-permute-done.3
  77.3 4.4 %collective-permute-done.4 = bf16[1,1,16,2,2048]{4,2,3,1,0:T(8,128)(2,1)S(1)} collective-permute-done((bf16[1,1,16,2,2048]{4,2,3,1,0:T(8,128)(2,1)S(1)}, bf16[1,1,16,2,2048]{4,2,3,1,0:T(8,128)(2,1)S(1)}, u32[]{:S(2)}, u32[]{:S(2)}) %collective-permute-start.4) | collective-permute-done | bytes 131104 | tf_op jit(solution)/shard_map/ppermute | solution.py:56
  81.6 0.3 fusion.28
  81.9 0.5 fusion.77
  82.4 2.1 %multiply_reduce_fusion = (f32[2,16]{1,0:T(2,128)S(1)}, f32[2,16,512]{2,1,0:T(8,128)S(1)}) fusion(bf16[2048,512]{1,0:T(8,128)(2,1)} %all-gather.5.cloned.1.call-done, f32[1,2,16,2,2048]{4,2,3,1,0:T(8,128)S(1)} %fusion.77), kind=kOutput, calls=%fused_computation.269 | convolution fusion | flops 67534816 | bytes 2687104 | tf_op jit(solution)/shard_map/frwj,jc->frwc/dot_general | solution.py:171
  84.5 0.1 fusion.182
  84.6 5.4 %all_gather.18 = bf16[4,2,16,512]{3,2,1,0:T(8,128)(2,1)S(1)} all-gather(bf16[1,2,16,512]{3,2,1,0:T(8,128)(2,1)S(1)} %fusion.182), channel_id=1, replica_groups=mesh['parts'=2,'row'=4,'frame'=4] {'frame'}, dimensions={0}, use_global_device_ids=true | all-gather | bytes 163840 | tf_op jit(solution)/shard_map/all_gather | solution.py:178
  90.0 3.8 %collective-permute-start.5 = (bf16[4,2,16,512]{3,2,1,0:T(8,128)(2,1)S(1)}, bf16[4,2,16,512]{3,2,1,0:T(8,128)(2,1)S(1)}, u32[]{:S(2)}, u32[]{:S(2)}) collective-permute-start(bf16[4,2,16,512]{3,2,1,0:T(8,128)(2,1)S(1)} %all_gather.18), channel_id=1, source_target_pairs={{0,4},{4,8},{8,12},{1,5},{5,9},{9,13},{2,6},{6,10},{10,14},{3,7},{... | collective-permute-start | bytes 393224 | tf_op jit(solution)/shard_map/ppermute | solution.py:54
  93.8 1.3 collective-permute-start.6
  95.1 1.9 %collective-permute-done.5 = bf16[4,2,16,512]{3,2,1,0:T(8,128)(2,1)S(1)} collective-permute-done((bf16[4,2,16,512]{3,2,1,0:T(8,128)(2,1)S(1)}, bf16[4,2,16,512]{3,2,1,0:T(8,128)(2,1)S(1)}, u32[]{:S(2)}, u32[]{:S(2)}) %collective-permute-start.5) | collective-permute-done | bytes 131104 | tf_op jit(solution)/shard_map/ppermute | solution.py:54
  97.1 4.1 %collective-permute-done.6 = bf16[4,2,16,512]{3,2,1,0:T(8,128)(2,1)S(1)} collective-permute-done((bf16[4,2,16,512]{3,2,1,0:T(8,128)(2,1)S(1)}, bf16[4,2,16,512]{3,2,1,0:T(8,128)(2,1)S(1)}, u32[]{:S(2)}, u32[]{:S(2)}) %collective-permute-start.6) | collective-permute-done | bytes 131104 | tf_op jit(solution)/shard_map/ppermute | solution.py:56
  101.2 0.8 pad_slice_fusion.23
  102.0 0.2 fusion.215
  102.2 1.0 copy-done.6
  103.2 0.4 convolution_bitcast_fusion.8
  103.6 0.4 convolution_bitcast_fusion.7
  104.0 0.4 convolution_bitcast_fusion.6
  104.4 0.4 convolution_bitcast_fusion.5
  104.8 0.4 convolution_bitcast_fusion.4
  105.1 0.4 convolution_bitcast_fusion.3
  105.5 0.4 convolution_bitcast_fusion.2
  105.9 0.4 convolution_bitcast_fusion.1
  106.3 0.4 fusion.13
  106.7 0.1 multiply_convert_fusion.1
  106.7 6.1 %all_gather.19 = bf16[4,4,16,512]{3,2,1,0:T(8,128)(2,1)S(1)} all-gather(bf16[4,4,16,128]{3,2,1,0:T(8,128)(2,1)S(1)} %multiply_convert_fusion.1), channel_id=1, replica_groups=mesh['parts'=2,'row'=4,'frame'=4] {'frame'}, dimensions={3}, use_global_device_ids=true | all-gather | bytes 327680 | tf_op jit(solution)/shard_map/all_gather | solution.py:185
  112.8 0.3 pad_slice_fusion.47
  113.2 0.1 fusion.217
  113.3 0.3 convolution_bitcast_fusion.17
  113.6 0.3 convolution_bitcast_fusion.16
  113.8 0.3 convolution_bitcast_fusion.15
  114.1 0.3 convolution_bitcast_fusion.14
  114.4 0.3 convolution_bitcast_fusion.13
  114.6 0.3 convolution_bitcast_fusion.12
  114.9 0.3 convolution_bitcast_fusion.11
  115.2 0.3 convolution_bitcast_fusion.10
  115.5 0.3 fusion.21
  115.8 6.5 %all_to_all.18 = bf16[4,2,16,128]{3,1,0,2:T(2,128)(2,1)S(1)} all-to-all(bf16[4,2,16,128]{3,1,0,2:T(2,128)(2,1)S(1)} %copy.42), channel_id=1, replica_groups=mesh['parts'=2,'row'=4,'frame'=4] {'frame'}, dimensions={2} | all-to-all | bytes 65536 | tf_op jit(solution)/shard_map/all_to_all | solution.py:189
  122.4 0.6 all_to_all.16
  (42 shorter events, 0.5 us)
Async XLA Ops:
  6.5 5.1 %copy-start.1 = (bf16[3,128,512]{2,1,0:T(8,128)(2,1)S(1)}, bf16[3,128,512]{2,1,0:T(8,128)(2,1)}, u32[]{:S(2)}) copy-start(bf16[3,128,512]{2,1,0:T(8,128)(2,1)} %param.11) | copy-start | bytes 1179652
  6.5 5.1 %copy-start = (bf16[1,2,16,512]{3,2,1,0:T(8,128)(2,1)S(1)}, bf16[1,2,16,512]{3,2,1,0:T(8,128)(2,1)}, u32[]{:S(2)}) copy-start(bf16[1,2,16,512]{3,2,1,0:T(8,128)(2,1)} %param.10) | copy-start | bytes 98308
  6.5 5.4 %copy-start.3 = (bf16[128,512]{1,0:T(8,128)(2,1)S(1)}, bf16[128,512]{1,0:T(8,128)(2,1)}, u32[]{:S(2)}) copy-start(bf16[128,512]{1,0:T(8,128)(2,1)} %param.12) | copy-start | bytes 393220
  6.5 63.8 %all-gather.3.cloned.1.call-start = ((), (), s32[]{:S(2)}) async-start(), calls=%async_computation.1 | async-start | bytes 5242880 | tf_op jit(solution)/shard_map/all_gather | solution.py:165
  9.0 73.4 %all-gather.5.cloned.1.call-start = ((), (), s32[]{:S(2)}) async-start(), calls=%async_computation.2 | async-start | bytes 2621440 | tf_op jit(solution)/shard_map/all_gather | solution.py:174
  9.0 19.8 %collective-permute-start = (bf16[3,128,512]{2,1,0:T(8,128)(2,1)}, bf16[3,128,512]{2,1,0:T(8,128)(2,1)S(1)}, u32[]{:S(2)}, u32[]{:S(2)}) collective-permute-start(bf16[3,128,512]{2,1,0:T(8,128)(2,1)} %param.11), channel_id=1, source_target_pairs={{0,1},{1,2},{2,3},{3,0},{4,5},{5,6},{6,7},{7,4},{8,9},{9,10},{10,1... | collective-permute-start | bytes 1179656 | tf_op jit(solution)/shard_map/ppermute | solution.py:18
  9.6 19.9 %collective-permute-start.1 = (bf16[3,128,512]{2,1,0:T(8,128)(2,1)}, bf16[3,128,512]{2,1,0:T(8,128)(2,1)S(1)}, u32[]{:S(2)}, u32[]{:S(2)}) collective-permute-start(bf16[3,128,512]{2,1,0:T(8,128)(2,1)} %param.11), channel_id=1, source_target_pairs={{1,0},{2,1},{3,2},{0,3},{5,4},{6,5},{7,6},{4,7},{9,8},{10,9},{11,1... | collective-permute-start | bytes 1179656 | tf_op jit(solution)/shard_map/ppermute | solution.py:19
  11.9 58.3 %copy-start.4 = (f32[512]{0:T(512)S(1)}, f32[512]{0:T(512)}, u32[]{:S(2)}) copy-start(f32[512]{0:T(512)} %param.13) | copy-start | bytes 6148
  28.8 16.5 %collective-permute-start.2 = (bf16[3,128,512]{2,1,0:T(8,128)(2,1)S(1)}, bf16[3,128,512]{2,1,0:T(8,128)(2,1)S(1)}, u32[]{:S(2)}, u32[]{:S(2)}) collective-permute-start(bf16[3,128,512]{2,1,0:T(8,128)(2,1)S(1)} %collective-permute-done), channel_id=1, source_target_pairs={{0,1},{1,2},{2,3},{3,0},{4,5},{5,6},{6,7},{7,4},{8,9},{9,10},{10,1... | collective-permute-start | bytes 1179656 | tf_op jit(solution)/shard_map/ppermute | solution.py:37
  70.3 5.8 %copy-start.2 = (f32[3,3,2,2048]{3,2,1,0:T(2,128)S(1)}, f32[3,3,2,2048]{3,2,1,0:T(2,128)}, u32[]{:S(2)}) copy-start(f32[3,3,2,2048]{3,2,1,0:T(2,128)} %param.15) | copy-start | bytes 442372
  73.5 3.8 %collective-permute-start.3 = (bf16[1,1,16,2,2048]{4,2,3,1,0:T(8,128)(2,1)S(1)}, bf16[1,1,16,2,2048]{4,2,3,1,0:T(8,128)(2,1)S(1)}, u32[]{:S(2)}, u32[]{:S(2)}) collective-permute-start(bf16[1,1,16,2,2048]{4,2,3,1,0:T(8,128)(2,1)S(1)} %get-tuple-element.62), channel_id=1, source_target_pairs={{0,4},{4,8},{8,12},{1,5},{5,9},{9,13},{2,6},{6,10},{10,14},{3,7},{... | collective-permute-start | bytes 393224 | tf_op jit(solution)/shard_map/ppermute | solution.py:54
  74.8 6.9 %collective-permute-start.4 = (bf16[1,1,16,2,2048]{4,2,3,1,0:T(8,128)(2,1)S(1)}, bf16[1,1,16,2,2048]{4,2,3,1,0:T(8,128)(2,1)S(1)}, u32[]{:S(2)}, u32[]{:S(2)}) collective-permute-start(bf16[1,1,16,2,2048]{4,2,3,1,0:T(8,128)(2,1)S(1)} %get-tuple-element.63), channel_id=1, source_target_pairs={{4,0},{8,4},{12,8},{5,1},{9,5},{13,9},{6,2},{10,6},{14,10},{7,3},{... | collective-permute-start | bytes 393224 | tf_op jit(solution)/shard_map/ppermute | solution.py:56
  76.1 8.4 %copy-start.5 = (f32[512]{0:T(512)S(1)}, f32[512]{0:T(512)}, u32[]{:S(2)}) copy-start(f32[512]{0:T(512)} %param.17) | copy-start | bytes 6148
  90.0 7.0 %collective-permute-start.5 = (bf16[4,2,16,512]{3,2,1,0:T(8,128)(2,1)S(1)}, bf16[4,2,16,512]{3,2,1,0:T(8,128)(2,1)S(1)}, u32[]{:S(2)}, u32[]{:S(2)}) collective-permute-start(bf16[4,2,16,512]{3,2,1,0:T(8,128)(2,1)S(1)} %all_gather.18), channel_id=1, source_target_pairs={{0,4},{4,8},{8,12},{1,5},{5,9},{9,13},{2,6},{6,10},{10,14},{3,7},{... | collective-permute-start | bytes 393224 | tf_op jit(solution)/shard_map/ppermute | solution.py:54
  93.8 7.4 %collective-permute-start.6 = (bf16[4,2,16,512]{3,2,1,0:T(8,128)(2,1)S(1)}, bf16[4,2,16,512]{3,2,1,0:T(8,128)(2,1)S(1)}, u32[]{:S(2)}, u32[]{:S(2)}) collective-permute-start(bf16[4,2,16,512]{3,2,1,0:T(8,128)(2,1)S(1)} %all_gather.18), channel_id=1, source_target_pairs={{4,0},{8,4},{12,8},{5,1},{9,5},{13,9},{6,2},{10,6},{14,10},{7,3},{... | collective-permute-start | bytes 393224 | tf_op jit(solution)/shard_map/ppermute | solution.py:56
  101.2 2.0 %copy-start.6 = (bf16[3,3,3,128,512]{4,3,2,1,0:T(8,128)(2,1)S(1)}, bf16[3,3,3,128,512]{4,3,2,1,0:T(8,128)(2,1)}, u32[]{:S(2)}) copy-start(bf16[3,3,3,128,512]{4,3,2,1,0:T(8,128)(2,1)} %param.18) | copy-start | bytes 10616836
  106.3 7.0 %copy-start.7 = (bf16[3,3,3,128,512]{4,3,2,1,0:T(8,128)(2,1)S(1)}, bf16[3,3,3,128,512]{4,3,2,1,0:T(8,128)(2,1)}, u32[]{:S(2)}) copy-start(bf16[3,3,3,128,512]{4,3,2,1,0:T(8,128)(2,1)} %param.19) | copy-start | bytes 10616836
Sparse Core Ops, SparseCore 0:
  9.1 43.3 all-gather.2
  54.0 24.6 all-gather.4
